TPU v7x, 32 devices: a whole 2x2x4 slice. The times are simulated.
32 devices in a mesh: ia: 4 (over z), ja: 2 (over y), ka: 4 (over x, core).
Axes of the slice: x: 2, y: 2, z: 4, core: 2. Of those that a mesh axis runs over, the one named last changes fastest.
Arguments:
- tile_values: bfloat16 [768, 128], P(('ia', 'ja', 'ka')), may hold values from -0.59765625 to 0.59765625
- tile_rows: int32 [768, 128], P(('ia', 'ja', 'ka')), may hold values from 0 to 63
- tile_cols: int32 [768, 128], P(('ia', 'ja', 'ka')), may hold values from 0 to 2047
- tile_depths: int32 [768, 128], P(('ia', 'ja', 'ka')), may hold values from 0 to 1023
- tile_live: int32 [32, 8], P(('ia', 'ja', 'ka')), may hold values from 0 to 3, as said below
- factor_b: bfloat16 [16, 2, 2048], P(None, 'ja', ('ia', 'ka')), may hold values from -6 to 6
- factor_c: bfloat16 [16, 4, 1024], P(None, 'ka', ('ia', 'ja')), may hold values from -6 to 6
- proj: float32 [16, 256], replicated, may hold values from -0.375 to 0.375
Outputs:
- tucker_y: float32 [2048, 256], P(('ia', 'ja', 'ka'))
- gram: float32 [256, 256], replicated
- new_factor: float32 [16, 2048], P(None, ('ia', 'ja', 'ka'))
Inputs may be any that keep to these rules, and one draw needn't show every extreme that they name: tile_live[d, o] counts the live leading slots among the 3 slots that device d holds for the device at index o along ja+ka within its mode-1 block; in every draw there is an owner for which every device has all 3 slots live, and every device has some owner with all 3 slots live.
All inputs are finite; a program needn't handle non-finite values.
Results may differ from a plain program's by a relative error of at most 0.0041.
Values may be sent and summed in bfloat16 or wider, within the bound.
A program may use at most 64 MiB of HBM per device.

v0:
```python
import jax
import jax.numpy as jnp
from jax import lax
from jax.sharding import PartitionSpec as P

RANK = 16
ROWS_DEV = 64


def owner_block(scaled, depth_rows, target):
    kron_rows = (scaled[:, None] * depth_rows[None, :]).reshape(
        scaled.shape[0] * depth_rows.shape[0], -1
    )
    onehot = (target.reshape(1, -1) == lax.iota(jnp.int32, ROWS_DEV)[:, None]).astype(jnp.bfloat16)
    return lax.dot_general(
        onehot, kron_rows, (((1,), (1,)), ((), ())), preferred_element_type=jnp.float32
    )


def group_blocks(scaled, depth_rows, target, begin_slot, pair_size, slot_count):
    rank_size = scaled.shape[0]
    tile_width = scaled.shape[2]
    scaled_part = lax.dynamic_slice_in_dim(scaled, begin_slot, pair_size * slot_count, 1)
    depth_part = lax.dynamic_slice_in_dim(depth_rows, begin_slot, pair_size * slot_count, 1)
    target_part = lax.dynamic_slice_in_dim(target, begin_slot, pair_size * slot_count, 0)
    scaled_part = scaled_part.reshape(rank_size, pair_size, slot_count, tile_width)
    depth_part = depth_part.reshape(depth_rows.shape[0], pair_size, slot_count, tile_width)
    target_part = target_part.reshape(pair_size, slot_count, tile_width)
    return jax.vmap(owner_block, in_axes=(1, 1, 0))(scaled_part, depth_part, target_part)


def owner_total(scaled, depth_rows, target, groups, slot_count):
    pair_size = 2
    columns = scaled.shape[0] * depth_rows.shape[0]
    result = jnp.zeros((ROWS_DEV, columns), jnp.float32)

    def turn(turn_index, result):
        begin_slot = turn_index * pair_size * slot_count
        blocks = group_blocks(scaled, depth_rows, target, begin_slot, pair_size, slot_count)
        return result + jnp.sum(blocks, axis=0)

    return lax.fori_loop(0, groups // pair_size, turn, result)


def on_device(tile_values, tile_rows, tile_cols, tile_depths, tile_live, factor_b, factor_c, proj):
    owners = lax.axis_size("ja") * lax.axis_size("ka")
    slot_total = tile_values.shape[0]
    slot_count = slot_total // owners
    mode_two = lax.all_gather(factor_b, ("ia", "ka"), axis=2, tiled=True)[:, 0, :]
    mode_three = lax.all_gather(factor_c, ("ia", "ja"), axis=2, tiled=True)[:, 0, :]
    slot_index = lax.iota(jnp.int32, slot_total)
    owner_of = slot_index // slot_count
    counts = jnp.sum(
        jnp.where(owner_of[:, None] == lax.iota(jnp.int32, owners)[None, :], tile_live, 0), axis=1
    )
    is_live = slot_index % slot_count < counts
    target = jnp.where(is_live[:, None], tile_rows, ROWS_DEV)
    scaled = (
        tile_values.astype(jnp.float32)[None]
        * jnp.take(mode_two, tile_cols, axis=1).astype(jnp.float32)
    ).astype(jnp.bfloat16)
    depth_rows = jnp.take(mode_three, tile_depths, axis=1)
    payload = jnp.concatenate([scaled, depth_rows], axis=0)
    arrived, routed = (
        lax.all_to_all(payload, ("ja", "ka"), split_axis=1, concat_axis=1, tiled=True),
        lax.all_to_all(target[None], ("ja", "ka"), split_axis=1, concat_axis=1, tiled=True),
    )
    summed = owner_total(arrived[:RANK], arrived[RANK:], routed[0], owners, slot_count)
    local_gram = lax.dot_general(
        summed,
        summed,
        (((0,), (0,)), ((), ())),
        precision=lax.Precision.HIGHEST,
        preferred_element_type=jnp.float32,
    )
    gram_total = lax.psum(local_gram, ("ia", "ja", "ka"))
    gram = gram_total / (ROWS_DEV * owners * lax.axis_size("ia"))
    new_factor = lax.dot_general(
        proj,
        summed,
        (((1,), (1,)), ((), ())),
        precision=lax.Precision.HIGHEST,
        preferred_element_type=jnp.float32,
    )
    return (summed, gram, new_factor)


def solution(mesh):
    return jax.shard_map(
        on_device,
        mesh=mesh,
        in_specs=(
            P(("ia", "ja", "ka"), None),
            P(("ia", "ja", "ka"), None),
            P(("ia", "ja", "ka"), None),
            P(("ia", "ja", "ka"), None),
            P(("ia", "ja", "ka"), None),
            P(None, "ja", ("ia", "ka")),
            P(None, "ka", ("ia", "ja")),
            P(),
        ),
        out_specs=(P(("ia", "ja", "ka"), None), P(), P(None, ("ia", "ja", "ka"))),
        check_vma=False,
    )
```

profile of v0, /device:TPU:0, one launch (start us, length us, event | category | flops | bytes accessed | tf_op | source)
XLA Modules:
  0.0 239.9 jit_solution(6678735856828618585)
XLA Ops:
  7.2 0.0 copy-start
  7.2 0.0 copy-start.2
  7.2 0.8 bitcast_clamp_fusion.1
  8.0 0.0 copy-done.2
  8.0 0.7 copy-done.3
  8.7 0.7 copy-done.6
  9.4 0.1 copy.29
  9.5 24.6 %all_gather.6 = bf16[16,1,2048]{0,2,1:T(8,128)(2,1)S(1)} all-gather(bf16[16,1,128]{0,2,1:T(8,128)(2,1)S(1)} %copy.29), channel_id=1, replica_groups=mesh['ia'=4,'ja'=2,'ka'=4] {'ia','ka'}, dimensions={2}, use_global_device_ids=true | all-gather | bytes 69632 | tf_op jit(solution)/shard_map/all_gather | solution.py:49
  34.1 9.2 %gather_fusion = bf16[3072,16]{1,0:T(8,128)(2,1)S(1)} fusion(bf16[16,2048]{0,1:T(8,128)(2,1)S(1)} %bitcast.41, s32[3072]{0:T(1024)S(1)} %bitcast_clamp_fusion.1), kind=kCustom, calls=%fused_computation | custom fusion | bytes 208896 | tf_op jit(solution)/shard_map/jit(_take)/gather | solution.py:60
  43.3 0.0 copy-start.5
  43.3 0.3 copy.30
  43.5 0.4 copy-done.5
  44.0 0.7 copy-done.7
  44.6 0.1 copy.31
  44.8 30.8 %all_gather.7 = bf16[16,1,1024]{0,2,1:T(8,128)(2,1)S(1)} all-gather(bf16[16,1,128]{0,2,1:T(8,128)(2,1)S(1)} %copy.31), channel_id=1, replica_groups=mesh['ia'=4,'ja'=2,'ka'=4] {'ia','ja'}, dimensions={2}, use_global_device_ids=true | all-gather | bytes 36864 | tf_op jit(solution)/shard_map/all_gather | solution.py:50
  75.5 9.2 %gather_fusion.1 = bf16[3072,16]{1,0:T(8,128)(2,1)S(1)} fusion(bf16[16,1024]{0,1:T(8,128)(2,1)S(1)} %bitcast.40, s32[3072]{0:T(1024)S(1)} %bitcast_clamp_fusion), kind=kCustom, calls=%fused_computation.1 | custom fusion | bytes 208896 | tf_op jit(solution)/shard_map/jit(_take)/gather | solution.py:62
  84.7 0.3 copy.32
  85.0 0.7 pad_maximum_fusion
  85.7 3.5 %all-to-all-start.1 = ((bf16[32,24,128]{2,0,1:T(8,128)(2,1)}), bf16[32,24,128]{2,0,1:T(8,128)(2,1)S(1)}, u32[]{:S(2)}, u32[]{:S(2)}) async-start(bf16[32,24,128]{2,0,1:T(8,128)(2,1)} %pad_maximum_fusion), calls=%async_computation.1 | async-start | bytes 393216 | tf_op jit(solution)/shard_map/all_to_all | solution.py:65
  89.3 0.0 copy-start.8
  89.3 0.6 copy-done.8
  90.0 0.1 select_reduce_fusion
  90.1 0.0 copy-done.4
  90.1 0.7 broadcast_select_fusion
  90.7 4.7 %all-to-all-done.1 = bf16[32,24,128]{2,0,1:T(8,128)(2,1)S(1)} async-done(((bf16[32,24,128]{2,0,1:T(8,128)(2,1)}), bf16[32,24,128]{2,0,1:T(8,128)(2,1)S(1)}, u32[]{:S(2)}, u32[]{:S(2)}) %all-to-all-start.1) | async-done | bytes 196640 | tf_op jit(solution)/shard_map/all_to_all | solution.py:65
  95.4 3.3 %all-to-all-start = ((s32[1,24,128]{2,0,1:T(1,128)}), s32[1,24,128]{2,0,1:T(1,128)S(1)}, u32[]{:S(2)}, u32[]{:S(2)}) async-start(s32[1,24,128]{2,0,1:T(1,128)} %bitcast.1), calls=%async_computation | async-start | bytes 24576 | tf_op jit(solution)/shard_map/all_to_all | solution.py:66
  98.7 0.0 all-reduce.2.cloned.1.call-start
  98.8 4.6 %all-to-all-done = s32[1,24,128]{2,0,1:T(1,128)S(1)} async-done(((s32[1,24,128]{2,0,1:T(1,128)}), s32[1,24,128]{2,0,1:T(1,128)S(1)}, u32[]{:S(2)}, u32[]{:S(2)}) %all-to-all-start) | async-done | bytes 12320 | tf_op jit(solution)/shard_map/all_to_all | solution.py:66
  103.4 3.7 %while.16 = (s32[]{:T(128)}, f32[64,256]{1,0:T(8,128)S(1)}, s32[24,128]{1,0:T(8,128)S(1)}, bf16[16,24,128]{2,0,1:T(8,128)(2,1)S(1)}, bf16[16,24,128]{2,0,1:T(8,1...) while((s32[]{:T(128)}, f32[64,256]{1,0:T(8,128)S(1)}, s32[24,128]{1,0:T(8,128)S(1)}, ...), condition=%wide.region_2.3_spmd.clone, body=%wide.region_1.2_spmd.clone.sunk | while | flops 25444360 | bytes 1965213 | solution.py:42
  103.5 0.2 broadcast_multiply_fusion.3
  103.7 0.3 mul.80
  104.0 0.3 fusion.14
  104.4 0.2 broadcast_multiply_fusion.3
  104.6 0.3 mul.80
  105.0 0.3 fusion.14
  105.3 0.2 broadcast_multiply_fusion.3
  105.5 0.3 mul.80
  105.9 0.3 fusion.14
  106.3 0.2 broadcast_multiply_fusion.3
  106.5 0.3 mul.80
  106.9 0.3 fusion.14
  107.1 0.0 copy-start.1
  107.2 1.1 fusion.5
  108.3 0.0 all-reduce.2.cloned.1.call-update
  108.3 0.0 copy-done.1
  108.3 0.8 convolution_bitcast_fusion.1
  109.1 122.3 %all-reduce.2.cloned.1.call-done = f32[256,256]{1,0:T(8,128)} async-done(((f32[256,256]{1,0:T(8,128)}), f32[256,256]{1,0:T(8,128)}) %all-reduce.2.cloned.1.call-update) | async-done | bytes 262160 | tf_op jit(solution)/shard_map/psum | solution.py:76
  231.4 1.7 broadcast_multiply_fusion.1
  (35 shorter events, 0.4 us)
Async XLA Ops:
  7.2 101.2 %copy-start = (f32[16,256]{1,0:T(8,128)S(1)}, f32[16,256]{1,0:T(8,128)}, u32[]{:S(2)}) copy-start(f32[16,256]{1,0:T(8,128)} %param.17) | copy-start | bytes 49156
  7.2 0.8 copy-start.2
  8.0 0.7 copy-start.3
  8.7 0.7 copy-start.6
  43.3 0.7 copy-start.5
  44.0 0.7 copy-start.7
  85.7 4.3 %copy-start.4 = (s32[24,128]{1,0:T(8,128)S(1)}, s32[24,128]{1,0:T(8,128)}, u32[]{:S(2)}) copy-start(s32[24,128]{1,0:T(8,128)} %param.11) | copy-start | bytes 36868
  85.7 9.7 %all-to-all-start.1 = ((bf16[32,24,128]{2,0,1:T(8,128)(2,1)}), bf16[32,24,128]{2,0,1:T(8,128)(2,1)S(1)}, u32[]{:S(2)}, u32[]{:S(2)}) async-start(bf16[32,24,128]{2,0,1:T(8,128)(2,1)} %pad_maximum_fusion), calls=%async_computation.1 | async-start | bytes 393216 | tf_op jit(solution)/shard_map/all_to_all | solution.py:65
  89.3 0.7 copy-start.8
  95.4 8.0 %all-to-all-start = ((s32[1,24,128]{2,0,1:T(1,128)}), s32[1,24,128]{2,0,1:T(1,128)S(1)}, u32[]{:S(2)}, u32[]{:S(2)}) async-start(s32[1,24,128]{2,0,1:T(1,128)} %bitcast.1), calls=%async_computation | async-start | bytes 24576 | tf_op jit(solution)/shard_map/all_to_all | solution.py:66
  98.7 132.6 %all-reduce.2.cloned.1.call-start = ((), (), s32[]{:S(2)}) async-start(), calls=%async_computation.2 | async-start | bytes 524288 | tf_op jit(solution)/shard_map/psum | solution.py:76
  107.1 1.2 copy-start.1
Sparse Core Ops, SparseCore 0:
  108.4 122.8 all-reduce.1
where the time goes:
time: 240 us
  waiting for transfers between devices  132 us (55%)
  blocking collectives  55.4 us (23%)
  local copies, waits for them, and re-layouts  23.8 us (10%)
  between operations  14.2 us (6%)
  starting transfers between devices  6.9 us (3%)
  other arithmetic  4.78 us (2%)
  matrix products  2.99 us (1%)
    psum x1, waiting for transfers between devices, on_device(): gram_total = lax.psum(local_gram, ('ia', 'ja', 'ka'))  122 us
    all_gather x1, blocking collectives, on_device(): lax.all_gather(factor_c, ('ia', 'ja'), axis=2, tiled=True)[:, 0, :]  30.8 us
    all_gather x1, blocking collectives, on_device(): lax.all_gather(factor_b, ('ia', 'ka'), axis=2, tiled=True)[:, 0, :]  24.6 us
    gather x2, local copies, waits for them, and re-layouts, on_device(): depth_rows = jnp.take(mode_three, tile_depths, axis=1)  9.41 us
    gather x2, local copies, waits for them, and re-layouts, on_device(): jnp.take(mode_two, tile_cols, axis=1).astype(jnp.float32)  9.41 us
  transfers between devices with their start and end apart: 3, of which 3 were waited for; matrix products, arithmetic and copies ran while one was open for 1% of the time, Pallas kernels for 0%

commit v1 on v0

--- a/solution.py
+++ b/solution.py
@@ -73,7 +73,7 @@
         precision=lax.Precision.HIGHEST,
         preferred_element_type=jnp.float32,
     )
-    gram_total = lax.psum(local_gram, ("ia", "ja", "ka"))
+    gram_total = jnp.sum(lax.all_gather(local_gram, ("ia", "ja", "ka")), axis=0)
     gram = gram_total / (ROWS_DEV * owners * lax.axis_size("ia"))
     new_factor = lax.dot_general(
         proj,

time: 240 us -> 196 us (0.82)
  waiting for transfers between devices: 132 us -> 81.3 us
  other arithmetic: 4.78 us -> 11.9 us
    psum x1 -> x0, waiting for transfers between devices: 122 us -> none  [on_device(): gram_total = lax.psum(local_gram, ('ia', 'ja', 'ka'))]
    all_gather x0 -> x1, waiting for transfers between devices: none -> 72.7 us  [on_device(): gram_total = jnp.sum(lax.all_gather(local_gram, ('ia', 'ja', 'ka')), axis=0)]
    reduce_sum x0 -> x1, other arithmetic: none -> 3.93 us  [on_device(): gram_total = jnp.sum(lax.all_gather(local_gram, ('ia', 'ja', 'ka')), axis=0)]
  transfers between devices with their start and end apart: 3 -> 3, of which waited for: 3 -> 3; matrix products, arithmetic and copies ran while one was open for 1% -> 2% of each run, Pallas kernels for 0% -> 0%
where the time goes in v1:
time: 196 us; the launch traced here: 195 us
  waiting for transfers between devices  81.3 us (41%)
  blocking collectives  55.4 us (28%)
  local copies, waits for them, and re-layouts  22 us (11%)
  between operations  14.1 us (7%)
  other arithmetic  11.9 us (6%)
  starting transfers between devices  6.77 us (3%)
  matrix products  2.99 us (2%)
    all_gather x1, waiting for transfers between devices, on_device(): gram_total = jnp.sum(lax.all_gather(local_gram, ('ia', 'ja', 'ka')), axis=0)  72.7 us
    all_gather x1, blocking collectives, on_device(): lax.all_gather(factor_c, ('ia', 'ja'), axis=2, tiled=True)[:, 0, :]  30.8 us
    all_gather x1, blocking collectives, on_device(): lax.all_gather(factor_b, ('ia', 'ka'), axis=2, tiled=True)[:, 0, :]  24.6 us
    gather x2, local copies, waits for them, and re-layouts, on_device(): depth_rows = jnp.take(mode_three, tile_depths, axis=1)  9.41 us
    gather x2, local copies, waits for them, and re-layouts, on_device(): jnp.take(mode_two, tile_cols, axis=1).astype(jnp.float32)  9.41 us
    all_to_all x1, waiting for transfers between devices, on_device(): lax.all_to_all(target[None], ('ja', 'ka'), split_axis=1, concat_axis=1, t...  4.59 us
    all_to_all x1, waiting for transfers between devices, on_device(): lax.all_to_all(payload, ('ja', 'ka'), split_axis=1, concat_axis=1, tiled=...  3.98 us
    reduce_sum x1, other arithmetic, on_device(): gram_total = jnp.sum(lax.all_gather(local_gram, ('ia', 'ja', 'ka')), axis=0)  3.93 us
  transfers between devices with their start and end apart: 3, of which 3 were waited for; matrix products, arithmetic and copies ran while one was open for 2% of the time, Pallas kernels for 0%

profile of v1, /device:TPU:0, one launch (start us, length us, event | category | flops | bytes accessed | tf_op | source)
XLA Modules:
  0.0 194.8 jit_solution(6732461057492195418)
XLA Ops:
  7.2 0.0 copy-start
  7.2 0.7 bitcast_clamp_fusion.1
  7.9 0.7 compare_and_fusion.1
  8.6 0.7 bitcast_clamp_fusion
  9.3 0.7 compare_and_fusion
  10.0 0.8 copy.29
  10.8 24.6 %all_gather.12 = bf16[16,1,2048]{0,2,1:T(8,128)(2,1)S(1)} all-gather(bf16[16,1,128]{0,2,1:T(8,128)(2,1)S(1)} %copy.29), channel_id=1, replica_groups=mesh['ia'=4,'ja'=2,'ka'=4] {'ia','ka'}, dimensions={2}, use_global_device_ids=true | all-gather | bytes 69632 | tf_op jit(solution)/shard_map/all_gather | solution.py:49
  35.4 9.2 %gather_fusion = bf16[3072,16]{1,0:T(8,128)(2,1)S(1)} fusion(bf16[16,2048]{0,1:T(8,128)(2,1)S(1)} %bitcast.43, s32[3072]{0:T(1024)S(1)} %bitcast_clamp_fusion.1), kind=kCustom, calls=%fused_computation | custom fusion | bytes 208896 | tf_op jit(solution)/shard_map/jit(_take)/gather | solution.py:60
  44.6 0.3 copy.30
  44.9 0.7 convert_element_type.12
  45.6 0.8 copy.31
  46.4 30.8 %all_gather.13 = bf16[16,1,1024]{0,2,1:T(8,128)(2,1)S(1)} all-gather(bf16[16,1,128]{0,2,1:T(8,128)(2,1)S(1)} %copy.31), channel_id=1, replica_groups=mesh['ia'=4,'ja'=2,'ka'=4] {'ia','ja'}, dimensions={2}, use_global_device_ids=true | all-gather | bytes 36864 | tf_op jit(solution)/shard_map/all_gather | solution.py:50
  77.1 9.2 %gather_fusion.1 = bf16[3072,16]{1,0:T(8,128)(2,1)S(1)} fusion(bf16[16,1024]{0,1:T(8,128)(2,1)S(1)} %bitcast.42, s32[3072]{0:T(1024)S(1)} %bitcast_clamp_fusion), kind=kCustom, calls=%fused_computation.1 | custom fusion | bytes 208896 | tf_op jit(solution)/shard_map/jit(_take)/gather | solution.py:62
  86.3 0.3 copy.32
  86.6 0.7 pad_maximum_fusion
  87.3 3.4 %all-to-all-start.1 = ((bf16[32,24,128]{2,0,1:T(8,128)(2,1)}), bf16[32,24,128]{2,0,1:T(8,128)(2,1)S(1)}, u32[]{:S(2)}, u32[]{:S(2)}) async-start(bf16[32,24,128]{2,0,1:T(8,128)(2,1)} %pad_maximum_fusion), calls=%async_computation.1 | async-start | bytes 393216 | tf_op jit(solution)/shard_map/all_to_all | solution.py:65
  90.8 0.7 select_reduce_fusion
  91.5 1.4 broadcast_select_fusion
  92.9 4.0 %all-to-all-done.1 = bf16[32,24,128]{2,0,1:T(8,128)(2,1)S(1)} async-done(((bf16[32,24,128]{2,0,1:T(8,128)(2,1)}), bf16[32,24,128]{2,0,1:T(8,128)(2,1)S(1)}, u32[]{:S(2)}, u32[]{:S(2)}) %all-to-all-start.1) | async-done | bytes 196640 | tf_op jit(solution)/shard_map/all_to_all | solution.py:65
  96.9 3.3 %all-to-all-start = ((s32[1,24,128]{2,0,1:T(1,128)}), s32[1,24,128]{2,0,1:T(1,128)S(1)}, u32[]{:S(2)}, u32[]{:S(2)}) async-start(s32[1,24,128]{2,0,1:T(1,128)} %bitcast.1), calls=%async_computation | async-start | bytes 24576 | tf_op jit(solution)/shard_map/all_to_all | solution.py:66
  100.2 0.0 all-gather.3.cloned.1.call-start
  100.3 4.6 %all-to-all-done = s32[1,24,128]{2,0,1:T(1,128)S(1)} async-done(((s32[1,24,128]{2,0,1:T(1,128)}), s32[1,24,128]{2,0,1:T(1,128)S(1)}, u32[]{:S(2)}, u32[]{:S(2)}) %all-to-all-start) | async-done | bytes 12320 | tf_op jit(solution)/shard_map/all_to_all | solution.py:66
  104.9 3.7 %while.16 = (s32[]{:T(128)}, f32[64,256]{1,0:T(8,128)S(1)}, s32[24,128]{1,0:T(8,128)S(1)}, bf16[16,24,128]{2,0,1:T(8,128)(2,1)S(1)}, bf16[16,24,128]{2,0,1:T(8,1...) while((s32[]{:T(128)}, f32[64,256]{1,0:T(8,128)S(1)}, s32[24,128]{1,0:T(8,128)S(1)}, ...), condition=%wide.region_2.3_spmd.clone, body=%wide.region_1.2_spmd.clone.sunk | while | flops 25444360 | bytes 1965213 | solution.py:42
  104.9 0.2 broadcast_multiply_fusion.3
  105.1 0.3 mul.80
  105.5 0.3 fusion.14
  105.9 0.2 broadcast_multiply_fusion.3
  106.1 0.3 mul.80
  106.5 0.3 fusion.14
  106.8 0.2 broadcast_multiply_fusion.3
  107.0 0.3 mul.80
  107.4 0.3 fusion.14
  107.8 0.2 broadcast_multiply_fusion.3
  108.0 0.3 mul.80
  108.3 0.3 fusion.14
  108.6 0.0 copy-start.1
  108.6 1.1 fusion.5
  109.8 0.0 all-gather.3.cloned.1.call-update
  109.8 0.0 copy-done
  109.8 0.8 convolution_bitcast_fusion.1
  110.6 72.7 %all-gather.3.cloned.1.call-done = f32[8192,256]{1,0:T(8,128)} async-done(((f32[256,256]{1,0:T(8,128)}), f32[8192,256]{1,0:T(8,128)}) %all-gather.3.cloned.1.call-update) | async-done | bytes 8388624 | tf_op jit(solution)/shard_map/all_gather | solution.py:76
  183.3 3.9 %reduce_sum.25 = f32[256,256]{1,0:T(8,128)S(1)} reduce(f32[32,256,256]{2,1,0:T(8,128)} %bitcast.41, f32[]{:T(128)} %constant.98.clone.1), dimensions={0}, to_apply=%region_3.4 | reduce | flops 2031616 | bytes 8650756 | tf_op jit(solution)/shard_map/reduce_sum | solution.py:76
  187.2 0.7 broadcast_multiply_fusion.1
  188.0 0.0 copy-done.1
  (26 shorter events, 0.3 us)
Async XLA Ops:
  7.2 102.6 %copy-start = (f32[16,256]{1,0:T(8,128)S(1)}, f32[16,256]{1,0:T(8,128)}, u32[]{:S(2)}) copy-start(f32[16,256]{1,0:T(8,128)} %param.17) | copy-start | bytes 49156
  87.3 9.5 %all-to-all-start.1 = ((bf16[32,24,128]{2,0,1:T(8,128)(2,1)}), bf16[32,24,128]{2,0,1:T(8,128)(2,1)S(1)}, u32[]{:S(2)}, u32[]{:S(2)}) async-start(bf16[32,24,128]{2,0,1:T(8,128)(2,1)} %pad_maximum_fusion), calls=%async_computation.1 | async-start | bytes 393216 | tf_op jit(solution)/shard_map/all_to_all | solution.py:65
  96.9 8.0 %all-to-all-start = ((s32[1,24,128]{2,0,1:T(1,128)}), s32[1,24,128]{2,0,1:T(1,128)S(1)}, u32[]{:S(2)}, u32[]{:S(2)}) async-start(s32[1,24,128]{2,0,1:T(1,128)} %bitcast.1), calls=%async_computation | async-start | bytes 24576 | tf_op jit(solution)/shard_map/all_to_all | solution.py:66
  100.2 83.1 %all-gather.3.cloned.1.call-start = ((), (), s32[]{:S(2)}) async-start(), calls=%async_computation.2 | async-start | bytes 8650752 | tf_op jit(solution)/shard_map/all_gather | solution.py:76
  108.6 79.3 %copy-start.1 = (f32[64,256]{1,0:T(8,128)}, f32[64,256]{1,0:T(8,128)S(1)}, u32[]{:S(2)}) copy-start(f32[64,256]{1,0:T(8,128)S(1)} %get-tuple-element.132) | copy-start | bytes 196612
Sparse Core Ops, SparseCore 0:
  109.9 73.3 all-gather.2
